TPU v7x, 32 devices: a whole 2x2x4 slice. The times are simulated.
32 devices in a mesh: seq: 4 (over y, core), chan: 8 (over z, x).
Axes of the slice: x: 2, y: 2, z: 4, core: 2. Of those that a mesh axis runs over, the one named last changes fastest.
Arguments:
- scan_input: bfloat16 [1024, 5120], P('seq', 'chan'), may hold values from -6 to 6
- gate_input: bfloat16 [1024, 5120], P('seq', 'chan'), may hold values from -6 to 6
- step_raw: bfloat16 [1024, 5120], P('seq', 'chan')
- log_rates: float32 [16, 5120], P(None, 'chan')
- skip_gain: float32 [5120], P('chan'), may hold values from 0.5 to 1.5
- state_write: float32 [16, 1024], P(None, 'seq'), may hold values from -6 to 6
- state_read: float32 [16, 1024], P(None, 'seq'), may hold values from -6 to 6
- out_weight: bfloat16 [5120, 2560], P('chan'), may hold values from -0.078125 to 0.078125
- out_cotangent: bfloat16 [1024, 2560], P('seq', 'chan'), may hold values from -6 to 6
Outputs:
- grad_input: bfloat16 [1024, 5120], P('seq', 'chan')
- grad_gate: bfloat16 [1024, 5120], P('seq', 'chan')
- grad_step: bfloat16 [1024, 5120], P('seq', 'chan')
- grad_rates: float32 [16, 5120], P(None, 'chan')
- grad_skip: float32 [5120], P('chan')
- grad_write: float32 [16, 1024], P(None, ('seq', 'chan'))
- grad_read: float32 [16, 1024], P(None, ('seq', 'chan'))
- grad_weight: float32 [5120, 2560], P('chan', 'seq')
All inputs are finite; a program needn't handle non-finite values.
Results may differ from a plain program's by a relative error of at most 0.0095.
Values may be sent and summed in bfloat16 or wider, within the bound.
A program may use at most 64 MiB of HBM per device.

v0:
```python
import functools

import jax
import jax.numpy as jnp
from jax import lax
from jax.experimental import pallas as pl
from jax.experimental.pallas import tpu as pltpu
from jax.sharding import PartitionSpec as P

CHUNK = 16
LANES = 128
LOG2E = 1.4426950408889634


def lane_groups(width):
    return [(lo, min(lo + LANES, width)) for lo in range(0, width, LANES)]


def softplus(raw):
    return jnp.maximum(raw, 0.0) + jnp.log1p(jnp.exp(-jnp.abs(raw)))


def sigmoid(value):
    return 1.0 / (1.0 + jnp.exp(-value))


def chunk_mask(rows, cols, states):
    row = lax.broadcasted_iota(jnp.int32, (rows, cols), 0)
    col = lax.broadcasted_iota(jnp.int32, (rows, cols), 1)
    return row == col // states


def wide(row, states):
    return jnp.broadcast_to(row, (states, row.shape[1]))


def end_kernel(raw_ref, x_ref, a2_ref, b_ref, out_ref, delta_s, dx_s, h_s, sum_s):
    states, width = h_s.shape
    block = raw_ref.shape[0]

    @pl.when(pl.program_id(0) == 0)
    def _():
        h_s[...] = jnp.zeros_like(h_s)
        sum_s[...] = jnp.zeros_like(sum_s)

    def chunk(c, _):
        base = pl.multiple_of(c * CHUNK, CHUNK)
        tok = pl.ds(base, CHUNK)
        delta = softplus(raw_ref[tok, :].astype(jnp.float32))
        delta_s[...] = delta
        dx_s[...] = delta * x_ref[tok, :].astype(jnp.float32)
        sum_s[...] += jnp.broadcast_to(jnp.sum(delta, axis=0, keepdims=True), sum_s.shape)
        for lo, hi in lane_groups(width):
            h = h_s[:, lo:hi]
            a2 = a2_ref[:, lo:hi]
            for k in range(CHUNK):
                d = wide(delta_s[k : k + 1, lo:hi], states)
                dx = wide(dx_s[k : k + 1, lo:hi], states)
                b = b_ref[pl.ds(pl.multiple_of((base + k) * states, states), states), : hi - lo]
                h = jnp.exp2(d * a2) * h + b * dx
            h_s[:, lo:hi] = h
        return 0

    lax.fori_loop(0, block // CHUNK, chunk, 0)

    @pl.when(pl.program_id(0) == pl.num_programs(0) - 1)
    def _():
        out_ref[:states] = h_s[...]
        out_ref[states:] = sum_s[...]


def forward_kernel(
    raw_ref, x_ref, gate_ref, dg_ref, a2_ref, b_ref, c_ref, cm_ref, skip_ref, hin_ref,
    gated_ref, ggate_ref, hprev_ref, read_ref, first_ref, gskip_ref,
    delta_s, dx_s, dy_s, hs_s, h_s, p_s, acc_s,
):
    states, width = h_s.shape
    block = raw_ref.shape[0]

    @pl.when(pl.program_id(0) == 0)
    def _():
        h_s[...] = hin_ref[...]
        p_s[...] = jnp.ones_like(p_s)
        acc_s[...] = jnp.zeros_like(acc_s)
        gskip_ref[...] = jnp.zeros_like(gskip_ref)

    mask = chunk_mask(CHUNK, CHUNK * states, states)

    def chunk(c, _):
        base = pl.multiple_of(c * CHUNK, CHUNK)
        tok = pl.ds(base, CHUNK)
        delta = softplus(raw_ref[tok, :].astype(jnp.float32))
        xf = x_ref[tok, :].astype(jnp.float32)
        delta_s[...] = delta
        dx_s[...] = delta * xf
        z = gate_ref[tok, :].astype(jnp.float32)
        s = sigmoid(z)
        dy = dg_ref[tok, :] * (z * s)
        dy_s[...] = dy
        gskip_ref[...] += jnp.sum(dy * xf, axis=0, keepdims=True)
        for lo, hi in lane_groups(width):
            h = h_s[:, lo:hi]
            p = p_s[:, lo:hi]
            acc = acc_s[:, lo:hi]
            a2 = a2_ref[:, lo:hi]
            hb = h.astype(jnp.bfloat16)
            for k in range(CHUNK):
                rows = pl.ds(pl.multiple_of((base + k) * states, states), states)
                d = wide(delta_s[k : k + 1, lo:hi], states)
                dx = wide(dx_s[k : k + 1, lo:hi], states)
                dyr = wide(dy_s[k : k + 1, lo:hi], states)
                hprev_ref[rows, lo:hi] = hb
                decay = jnp.exp2(d * a2)
                h = decay * h + b_ref[rows, : hi - lo] * dx
                hb = h.astype(jnp.bfloat16)
                hs_s[k * states : (k + 1) * states, lo:hi] = hb
                p = p * decay
                acc = acc + p * (c_ref[rows, : hi - lo] * dyr)
            h_s[:, lo:hi] = h
            p_s[:, lo:hi] = p
            acc_s[:, lo:hi] = acc
        hs = hs_s[...]
        y = jnp.dot(cm_ref[tok, :], hs, preferred_element_type=jnp.float32)
        y = y + skip_ref[...] * x_ref[tok, :].astype(jnp.float32)
        read = lax.dot_general(
            dy_s[...].astype(jnp.bfloat16), hs, (((1,), (1,)), ((), ())),
            preferred_element_type=jnp.float32,
        )
        read_ref[c] = jnp.sum(jnp.where(mask, read, 0.0), axis=0, keepdims=True)
        z = gate_ref[tok, :].astype(jnp.float32)
        s = sigmoid(z)
        gated_ref[tok, :] = (y * (z * s)).astype(jnp.bfloat16)
        ggate_ref[tok, :] = (dg_ref[tok, :] * y * s * (1.0 + z * (1.0 - s))).astype(jnp.bfloat16)
        return 0

    lax.fori_loop(0, block // CHUNK, chunk, 0)

    @pl.when(pl.program_id(0) == pl.num_programs(0) - 1)
    def _():
        first_ref[...] = acc_s[...]


def back_kernel(
    raw_ref, x_ref, gate_ref, dg_ref, a2_ref, a_ref, c_ref, bm_ref, skip_ref, hprev_ref, om_ref,
    gx_ref, gstep_ref, write_ref, rates_ref,
    delta_s, dx_s, dy_s, lam_s, wa_s, om_s, acc_s,
):
    states, width = om_s.shape
    block = raw_ref.shape[0]

    @pl.when(pl.program_id(0) == 0)
    def _():
        om_s[...] = om_ref[...]
        acc_s[...] = jnp.zeros_like(acc_s)

    mask = chunk_mask(CHUNK, CHUNK * states, states)
    ones = mask.astype(jnp.float32).astype(jnp.bfloat16)
    nchunks = block // CHUNK

    def chunk(i, _):
        c = nchunks - 1 - i
        base = pl.multiple_of(c * CHUNK, CHUNK)
        tok = pl.ds(base, CHUNK)
        delta = softplus(raw_ref[tok, :].astype(jnp.float32))
        delta_s[...] = delta
        dx_s[...] = delta * x_ref[tok, :].astype(jnp.float32)
        z = gate_ref[tok, :].astype(jnp.float32)
        dy_s[...] = dg_ref[tok, :] * (z * sigmoid(z))
        for lo, hi in lane_groups(width):
            om = om_s[:, lo:hi]
            acc = acc_s[:, lo:hi]
            a2 = a2_ref[:, lo:hi]
            a = a_ref[:, lo:hi]
            for k in reversed(range(CHUNK)):
                rows = pl.ds(pl.multiple_of((base + k) * states, states), states)
                d = wide(delta_s[k : k + 1, lo:hi], states)
                dyr = wide(dy_s[k : k + 1, lo:hi], states)
                lam = c_ref[rows, : hi - lo] * dyr + om
                lam_s[k * states : (k + 1) * states, lo:hi] = lam.astype(jnp.bfloat16)
                om = jnp.exp2(d * a2) * lam
                w = om * hprev_ref[rows, lo:hi].astype(jnp.float32)
                wa_s[k * states : (k + 1) * states, lo:hi] = (w * a).astype(jnp.bfloat16)
                acc = acc + w * d
            om_s[:, lo:hi] = om
            acc_s[:, lo:hi] = acc
        lam_all = lam_s[...]
        lam_b = jnp.dot(bm_ref[tok, :], lam_all, preferred_element_type=jnp.float32)
        rate = jnp.dot(ones, wa_s[...], preferred_element_type=jnp.float32)
        write = lax.dot_general(
            dx_s[...].astype(jnp.bfloat16), lam_all, (((1,), (1,)), ((), ())),
            preferred_element_type=jnp.float32,
        )
        write_ref[c] = jnp.sum(jnp.where(mask, write, 0.0), axis=0, keepdims=True)
        gdelta = x_ref[tok, :].astype(jnp.float32) * lam_b + rate
        gstep_ref[tok, :] = (gdelta * sigmoid(raw_ref[tok, :].astype(jnp.float32))).astype(jnp.bfloat16)
        gx_ref[tok, :] = (delta_s[...] * lam_b + dy_s[...] * skip_ref[...]).astype(jnp.bfloat16)
        return 0

    lax.fori_loop(0, nchunks, chunk, 0)

    @pl.when(pl.program_id(0) == pl.num_programs(0) - 1)
    def _():
        rates_ref[...] = acc_s[...] * a_ref[...]


def on_device(
    scan_input, gate_input, step_raw, log_rates, skip_gain,
    state_write, state_read, out_weight, out_cotangent,
):
    tokens, width = scan_input.shape
    states = log_rates.shape[0]
    block = min(64, tokens)
    nblocks = tokens // block
    f32, bf16 = jnp.float32, jnp.bfloat16
    seq_devices = lax.axis_size("seq")
    me = lax.axis_index("seq")

    a_neg = -jnp.exp(log_rates)
    a2 = a_neg * LOG2E
    skip_row = skip_gain[None, :]
    b_rows, c_rows = state_write.T, state_read.T

    def lanes(rows):
        return jnp.broadcast_to(rows[:, :, None], (tokens, states, LANES)).reshape(tokens * states, LANES)

    def diagonal(rows):
        spread = jnp.tile(rows.astype(bf16), (1, CHUNK))
        place = (jnp.arange(CHUNK * states) // states)[None, :]
        return jnp.where(place == (jnp.arange(tokens) % CHUNK)[:, None], spread, jnp.zeros((), bf16))

    b_wide, c_wide = lanes(b_rows), lanes(c_rows)
    bm, cm = diagonal(b_rows), diagonal(c_rows)

    def specs(order):
        by_token = pl.BlockSpec((block, width), lambda i: (order(i), 0))
        by_state = pl.BlockSpec((block * states, LANES), lambda i: (order(i), 0))
        history = pl.BlockSpec((block * states, width), lambda i: (order(i), 0))
        diag = pl.BlockSpec((block, CHUNK * states), lambda i: (order(i), 0))
        sums = pl.BlockSpec((block // CHUNK, 1, CHUNK * states), lambda i: (order(i), 0, 0))
        return by_token, by_state, history, diag, sums

    state_spec = pl.BlockSpec((states, width), lambda i: (0, 0))
    row_spec = pl.BlockSpec((1, width), lambda i: (0, 0))
    params = pltpu.CompilerParams(dimension_semantics=("arbitrary",))
    token_scratch = pltpu.VMEM((CHUNK, width), f32)
    state_scratch = pltpu.VMEM((states, width), f32)
    chunk_scratch = pltpu.VMEM((CHUNK * states, width), bf16)
    volume = tokens * states * width

    def cost(scale):
        return pl.CostEstimate(flops=scale * volume, bytes_accessed=4 * volume, transcendentals=volume)

    by_token, by_state, history, diag, sums = specs(lambda i: i)
    pad = 8
    ending = pl.pallas_call(
        end_kernel,
        grid=(nblocks,),
        in_specs=[by_token, by_token, state_spec, by_state],
        out_specs=pl.BlockSpec((states + pad, width), lambda i: (0, 0)),
        out_shape=jax.ShapeDtypeStruct((states + pad, width), f32),
        scratch_shapes=[token_scratch, token_scratch, state_scratch, pltpu.VMEM((pad, width), f32)],
        compiler_params=params,
        cost_estimate=cost(5),
        name="ending",
    )(step_raw, scan_input, a2, b_wide)

    dout_full = lax.all_gather(out_cotangent, "chan", axis=1, tiled=True)
    endings = lax.all_gather(ending, "seq", axis=0)
    decays = jnp.exp2(endings[:, states : states + 1] * a2[None])
    h_in = jnp.zeros((states, width), f32)
    for j in range(seq_devices - 1):
        h_in = jnp.where(j < me, decays[j] * h_in + endings[j, :states], h_in)

    dg = lax.dot_general(dout_full, out_weight, (((1,), (1,)), ((), ())), preferred_element_type=f32)

    gated, grad_gate, hprev, read, first, skip_part = pl.pallas_call(
        forward_kernel,
        grid=(nblocks,),
        in_specs=[by_token] * 4 + [state_spec, by_state, by_state, diag, row_spec, state_spec],
        out_specs=[by_token, by_token, history, sums, state_spec, row_spec],
        out_shape=[
            jax.ShapeDtypeStruct((tokens, width), bf16),
            jax.ShapeDtypeStruct((tokens, width), bf16),
            jax.ShapeDtypeStruct((tokens * states, width), bf16),
            jax.ShapeDtypeStruct((tokens // CHUNK, 1, CHUNK * states), f32),
            jax.ShapeDtypeStruct((states, width), f32),
            jax.ShapeDtypeStruct((1, width), f32),
        ],
        scratch_shapes=[token_scratch] * 3 + [chunk_scratch] + [state_scratch] * 3,
        compiler_params=params,
        cost_estimate=cost(12),
        name="forward",
    )(step_raw, scan_input, gate_input, dg, a2, b_wide, c_wide, cm, skip_row, h_in)

    firsts = lax.all_gather(first, "seq", axis=0)
    gated_all = lax.all_gather(gated, "seq", axis=0, tiled=True)
    columns = lax.all_to_all(dout_full, "seq", split_axis=1, concat_axis=0, tiled=True)
    omega = jnp.zeros((states, width), f32)
    for j in reversed(range(1, seq_devices)):
        omega = jnp.where(j > me, decays[j] * omega + firsts[j], omega)

    by_token, by_state, history, diag, sums = specs(lambda i: nblocks - 1 - i)
    grad_input, grad_step, write, rates = pl.pallas_call(
        back_kernel,
        grid=(nblocks,),
        in_specs=[by_token] * 4
        + [state_spec, state_spec, by_state, diag, row_spec, history, state_spec],
        out_specs=[by_token, by_token, sums, state_spec],
        out_shape=[
            jax.ShapeDtypeStruct((tokens, width), bf16),
            jax.ShapeDtypeStruct((tokens, width), bf16),
            jax.ShapeDtypeStruct((tokens // CHUNK, 1, CHUNK * states), f32),
            jax.ShapeDtypeStruct((states, width), f32),
        ],
        scratch_shapes=[token_scratch] * 3 + [chunk_scratch] * 2 + [state_scratch] * 2,
        compiler_params=params,
        cost_estimate=cost(14),
        name="backward",
    )(step_raw, scan_input, gate_input, dg, a2, a_neg, c_wide, bm, skip_row, hprev, omega)

    both = jnp.concatenate([write.reshape(tokens, states).T, read.reshape(tokens, states).T], axis=0)
    both = lax.psum_scatter(both, "chan", scatter_dimension=1, tiled=True)
    grad_write, grad_read = both[:states], both[states:]
    sums_seq = lax.psum(jnp.concatenate([rates, skip_part], axis=0), "seq")
    grad_rates, grad_skip = sums_seq[:states], sums_seq[states]
    grad_weight = lax.dot_general(
        gated_all, columns, (((0,), (0,)), ((), ())), preferred_element_type=f32
    )
    return (
        grad_input, grad_gate, grad_step, grad_rates, grad_skip, grad_write, grad_read, grad_weight,
    )


def solution(mesh):
    return jax.shard_map(
        on_device,
        mesh=mesh,
        in_specs=(
            P("seq", "chan"),
            P("seq", "chan"),
            P("seq", "chan"),
            P(None, "chan"),
            P("chan"),
            P(None, "seq"),
            P(None, "seq"),
            P("chan", None),
            P("seq", "chan"),
        ),
        out_specs=(
            P("seq", "chan"),
            P("seq", "chan"),
            P("seq", "chan"),
            P(None, "chan"),
            P("chan"),
            P(None, ("seq", "chan")),
            P(None, ("seq", "chan")),
            P("chan", "seq"),
        ),
        check_vma=False,
    )
```

profile of v0, /device:TPU:0, one launch (start us, length us, event | category | flops | bytes accessed | tf_op | source)
XLA Modules:
  0.0 185.6 jit_solution(12067139557090872627)
XLA Ops:
  8.0 1.0 copy.41
  9.8 0.8 copy.44
  11.3 0.8 copy.42
  13.5 2.0 %broadcast_in_dim.34.b_ref = f32[4096,128]{1,0:T(8,128)} broadcast(f32[4096]{0:T(1024)S(1)} %broadcast_in_dim.33), dimensions={0} | broadcast | bytes 2113536 | tf_op jit(solution)/shard_map/broadcast_in_dim | solution.py:224
  15.5 4.9 %ending.1 = f32[24,640]{1,0:T(8,128)} custom-call(bf16[256,640]{1,0:T(8,128)(2,1)} %raw_ref.5, bf16[256,640]{1,0:T(8,128)(2,1)} %x_ref.5, f32[16,640]{1,0:T(8,128)} %get-tuple-element.45.a2_ref, f32[4096,128]{1,0:T(8,128)} %broadcast_in_dim.34.b_ref), custom_call_target="tpu_custom_call" | custom-call | flops 13107200 | bytes 10485760 | tf_op jit(solution)/shard_map/ending/pallas_call | solution.py:255
  20.4 7.4 %all-gather = f32[96,640]{1,0:T(8,128)S(1)} all-gather(f32[24,640]{1,0:T(8,128)} %ending.1), channel_id=2, replica_groups=mesh['seq'=4,'chan'=8] {'seq'}, dimensions={0}, use_global_device_ids=true | all-gather | bytes 307200 | tf_op jit(solution)/shard_map/all_gather | solution.py:268
  28.5 1.4 fusion.6.hin_ref
  30.0 1.8 compare_select_fusion
  31.8 23.0 %all-gather.5.cloned.1.call-done = bf16[256,2560]{0,1:T(8,128)(2,1)} async-done(((bf16[256,320]{0,1:T(8,128)(2,1)}), bf16[256,2560]{0,1:T(8,128)(2,1)}) %all-gather.5.cloned.1.call-update) | async-done | bytes 1310736 | tf_op jit(solution)/shard_map/all_gather | solution.py:267
  54.8 3.4 %fusion.14.dg_ref = f32[256,640]{1,0:T(8,128)} fusion(bf16[256,2560]{0,1:T(8,128)(2,1)} %all-gather.5.cloned.1.call-done, bf16[640,2560]{1,0:T(8,128)(2,1)S(1)} %copy-done), kind=kOutput, calls=%fused_computation.40 | convolution fusion | flops 838860800 | bytes 5242880 | tf_op jit(solution)/shard_map/dot_general | solution.py:274
  58.2 1.9 %broadcast_in_dim.30.c_ref = f32[4096,128]{1,0:T(8,128)} broadcast(f32[4096]{0:T(1024)S(1)} %broadcast_in_dim.15), dimensions={0} | broadcast | bytes 2113536 | tf_op jit(solution)/shard_map/broadcast_in_dim | solution.py:224
  60.1 11.2 %forward.1 = (bf16[256,640]{1,0:T(8,128)(2,1)}, bf16[256,640]{1,0:T(8,128)(2,1)}, bf16[4096,640]{1,0:T(8,128)(2,1)}, f32[16,1,256]{2,1,0:T(1,128)}, f32[16,640]{1,0:T(8,128)}, /*index=5*/f32[1,640]{1,0:T(1,128)}) custom-call(bf16[256,640]{1,0:T(8,128)(2,1)} %raw_ref.5, bf16[256,640]{1,0:T(8,128)(2,1)} %x_ref.5, bf16[256,640]{1,0:T(8,128)(2,1)} %gate_ref.3, ...), custom_call_target="tpu_custom_call" | custom-call | flops 31457280 | bytes 10485760 | tf_op jit(solution)/shard_map/forward/pallas_call | solution.py:276
  71.4 7.0 %all-gather.1 = f32[64,640]{1,0:T(8,128)} all-gather(f32[16,640]{1,0:T(8,128)} %get-tuple-element.19), channel_id=3, replica_groups=mesh['seq'=4,'chan'=8] {'seq'}, dimensions={0}, use_global_device_ids=true | all-gather | bytes 204800 | tf_op jit(solution)/shard_map/all_gather | solution.py:295
  79.9 1.0 copy.46
  80.8 1.5 fusion.om_ref
  82.3 12.1 %backward.1 = (bf16[256,640]{1,0:T(8,128)(2,1)}, bf16[256,640]{1,0:T(8,128)(2,1)}, f32[16,1,256]{2,1,0:T(1,128)}, f32[16,640]{1,0:T(8,128)}) custom-call(bf16[256,640]{1,0:T(8,128)(2,1)} %raw_ref.5, bf16[256,640]{1,0:T(8,128)(2,1)} %x_ref.5, bf16[256,640]{1,0:T(8,128)(2,1)} %gate_ref.3, f32[256,640]{1,0:T(8,128)} %fusion.14.dg_ref, ...), custom_call_target="tpu_custom_call" | custom-call | flops 36700160 | bytes 10485760 | tf_op jit(solution)/shard_map/backward/pallas_call | solution.py:303
  95.4 0.8 copy.48
  96.9 4.5 %all-to-all-start = ((bf16[256,4,640]{0,2,1:T(8,128)(2,1)}), bf16[256,4,640]{0,2,1:T(8,128)(2,1)}, u32[]{:S(2)}, u32[]{:S(2)}) async-start(bf16[256,4,640]{0,2,1:T(8,128)(2,1)} %bitcast.65), calls=%async_computation | async-start | bytes 2621440 | tf_op jit(solution)/shard_map/all_to_all | solution.py:297
  101.4 24.0 %psum.7 = f32[17,640]{1,0:T(8,128)S(1)} all-reduce(f32[17,640]{1,0:T(8,128)S(1)} %pad_maximum_fusion), channel_id=1, replica_groups=mesh['seq'=4,'chan'=8] {'seq'}, use_global_device_ids=true, to_apply=%region_0.1 | all-reduce | flops 10880 | bytes 87040 | tf_op jit(solution)/shard_map/psum | solution.py:324
  126.7 29.5 %reduce-scatter.4.cloned.1.call-done = f32[32,32]{1,0:T(8,128)} async-done(((f32[256,32]{1,0:T(8,128)}), f32[32,32]{1,0:T(8,128)}) %reduce-scatter.4.cloned.1.call-update) | async-done | bytes 4112
  156.2 0.9 fusion.13
  158.4 2.4 %copy.47 = bf16[4,256,640]{2,1,0:T(8,128)(2,1)} copy(bf16[4,256,640]{1,2,0:T(8,128)(2,1)} %bitcast.15) | data formatting | bytes 2621440 | tf_op jit(solution)/shard_map/all_to_all | solution.py:297
  160.8 14.1 %all-gather.7.cloned.1.call-done = bf16[1024,640]{1,0:T(8,128)(2,1)} async-done(((bf16[256,640]{1,0:T(8,128)(2,1)}), bf16[1024,640]{1,0:T(8,128)(2,1)}) %all-gather.7.cloned.1.call-update) | async-done | bytes 1310736 | tf_op jit(solution)/shard_map/all_gather | solution.py:296
  174.9 4.1 %fusion.15 = f32[640,640]{1,0:T(8,128)} fusion(bf16[1024,640]{1,0:T(8,128)(2,1)} %all-gather.7.cloned.1.call-done, bf16[1024,640]{1,0:T(8,128)(2,1)} %bitcast.66), kind=kOutput, calls=%fused_computation.41 | convolution fusion | flops 838860800 | bytes 4259840 | tf_op jit(solution)/shard_map/dot_general | solution.py:326
  (47 shorter events, 10.3 us)
Async XLA Ops:
  7.2 47.6 %copy-start = (bf16[640,2560]{1,0:T(8,128)(2,1)S(1)}, bf16[640,2560]{1,0:T(8,128)(2,1)}, u32[]{:S(2)}) copy-start(bf16[640,2560]{1,0:T(8,128)(2,1)} %param.16) | copy-start | bytes 9830404
  7.2 5.5 %copy-start.3 = (f32[16,256]{1,0:T(8,128)S(1)}, f32[16,256]{1,0:T(8,128)}, u32[]{:S(2)}) copy-start(f32[16,256]{1,0:T(8,128)} %param.14) | copy-start | bytes 49156
  7.2 4.9 %copy-start.6 = (f32[640]{0:T(1024)S(1)}, f32[640]{0:T(1024)}, u32[]{:S(2)}) copy-start(f32[640]{0:T(1024)} %param.13) | copy-start | bytes 7684
  7.2 5.7 %copy-start.5 = (f32[16,640]{1,0:T(8,128)S(1)}, f32[16,640]{1,0:T(8,128)}, u32[]{:S(2)}) copy-start(f32[16,640]{1,0:T(8,128)} %param.12) | copy-start | bytes 122884
  7.2 47.6 %all-gather.5.cloned.1.call-start = ((), (), s32[]{:S(2)}) async-start(), calls=%async_computation.2 | async-start | bytes 1474560 | tf_op jit(solution)/shard_map/all_gather | solution.py:267
  7.9 148.2 %reduce-scatter.4.cloned.1.call-start = ((), (), s32[]{:S(2)}) async-start(), calls=%async_computation.4 | async-start | bytes 147456
  15.5 13.0 %copy-start.1 = (f32[16,640]{1,0:T(8,128)S(1)}, f32[16,640]{1,0:T(8,128)}, u32[]{:S(2)}) copy-start(f32[16,640]{1,0:T(8,128)} %get-tuple-element.45.a2_ref) | copy-start | bytes 122884
  27.8 0.7 copy-start.2
  96.2 78.8 %all-gather.7.cloned.1.call-start = ((), (), s32[]{:S(2)}) async-start(), calls=%async_computation.3 | async-start | bytes 1638400 | tf_op jit(solution)/shard_map/all_gather | solution.py:296
  96.9 4.5 %copy-start.4 = (f32[16,640]{1,0:T(8,128)S(1)}, f32[16,640]{1,0:T(8,128)}, u32[]{:S(2)}) copy-start(f32[16,640]{1,0:T(8,128)} %get-tuple-element.23) | copy-start | bytes 122884
  96.9 4.5 %copy-start.7 = (f32[1,640]{1,0:T(1,128)S(1)}, f32[1,640]{1,0:T(1,128)}, u32[]{:S(2)}) copy-start(f32[1,640]{1,0:T(1,128)} %get-tuple-element.24) | copy-start | bytes 7684
  96.9 61.4 %all-to-all-start = ((bf16[256,4,640]{0,2,1:T(8,128)(2,1)}), bf16[256,4,640]{0,2,1:T(8,128)(2,1)}, u32[]{:S(2)}, u32[]{:S(2)}) async-start(bf16[256,4,640]{0,2,1:T(8,128)(2,1)} %bitcast.65), calls=%async_computation | async-start | bytes 2621440 | tf_op jit(solution)/shard_map/all_to_all | solution.py:297
Sparse Core Ops, SparseCore 0:
  10.2 44.5 all-gather.4
  96.3 59.8 reduce-scatter.3
  157.7 17.1 all-gather.6
where the time goes:
time: 187 us; the launch traced here: 186 us
  waiting for transfers between devices  68 us (36%)
  blocking collectives  38.4 us (21%)
  Pallas kernels  28.2 us (15%)
  local copies, waits for them, and re-layouts  16.6 us (9%)
  between operations  13.9 us (7%)
  other arithmetic  8.33 us (4%)
  matrix products  7.48 us (4%)
  starting transfers between devices  4.58 us (2%)
    unnamed x4, waiting for transfers between devices  30.9 us
    psum x1, blocking collectives, on_device(): sums_seq = lax.psum(jnp.concatenate([rates, skip_part], axis=0), 'seq')  24 us
    all_gather x1, waiting for transfers between devices, on_device(): dout_full = lax.all_gather(out_cotangent, 'chan', axis=1, tiled=True)  23 us
    all_gather x1, waiting for transfers between devices, on_device(): gated_all = lax.all_gather(gated, 'seq', axis=0, tiled=True)  14.1 us
    pallas_call x1, Pallas kernels, on_device(): pl.pallas_call(back_kernel, grid=(nblocks,), in_specs=[by_token] * 4 + [s...  12.1 us
    pallas_call x1, Pallas kernels, on_device(): pl.pallas_call(forward_kernel, grid=(nblocks,), in_specs=[by_token] * 4 +...  11.2 us
    all_gather x1, blocking collectives, on_device(): endings = lax.all_gather(ending, 'seq', axis=0)  7.37 us
    all_gather x1, blocking collectives, on_device(): firsts = lax.all_gather(first, 'seq', axis=0)  7 us
  transfers between devices with their start and end apart: 4, of which 3 were waited for; matrix products, arithmetic and copies ran while one was open for 9% of the time, Pallas kernels for 3%

commit v1 on v0

--- a/solution.py
+++ b/solution.py
@@ -22,6 +22,11 @@
 
 def sigmoid(value):
     return 1.0 / (1.0 + jnp.exp(-value))
+
+
+def from_all(array, axis):
+    copies = jnp.broadcast_to(array[None], (lax.axis_size(axis),) + array.shape)
+    return lax.all_to_all(copies, axis, split_axis=0, concat_axis=0, tiled=True)
 
 
 def chunk_mask(rows, cols, states):
@@ -264,8 +269,8 @@
         name="ending",
     )(step_raw, scan_input, a2, b_wide)
 
-    dout_full = lax.all_gather(out_cotangent, "chan", axis=1, tiled=True)
-    endings = lax.all_gather(ending, "seq", axis=0)
+    dout_full = jnp.swapaxes(from_all(out_cotangent, "chan"), 0, 1).reshape(tokens, -1)
+    endings = from_all(ending, "seq")
     decays = jnp.exp2(endings[:, states : states + 1] * a2[None])
     h_in = jnp.zeros((states, width), f32)
     for j in range(seq_devices - 1):
@@ -292,8 +297,8 @@
         name="forward",
     )(step_raw, scan_input, gate_input, dg, a2, b_wide, c_wide, cm, skip_row, h_in)
 
-    firsts = lax.all_gather(first, "seq", axis=0)
-    gated_all = lax.all_gather(gated, "seq", axis=0, tiled=True)
+    firsts = from_all(first, "seq")
+    gated_all = from_all(gated, "seq").reshape(-1, width)
     columns = lax.all_to_all(dout_full, "seq", split_axis=1, concat_axis=0, tiled=True)
     omega = jnp.zeros((states, width), f32)
     for j in reversed(range(1, seq_devices)):
@@ -319,9 +324,11 @@
     )(step_raw, scan_input, gate_input, dg, a2, a_neg, c_wide, bm, skip_row, hprev, omega)
 
     both = jnp.concatenate([write.reshape(tokens, states).T, read.reshape(tokens, states).T], axis=0)
-    both = lax.psum_scatter(both, "chan", scatter_dimension=1, tiled=True)
+    chan_devices = lax.axis_size("chan")
+    pieces = jnp.swapaxes(both.reshape(2 * states, chan_devices, -1), 0, 1)
+    both = jnp.sum(lax.all_to_all(pieces, "chan", split_axis=0, concat_axis=0, tiled=True), axis=0)
     grad_write, grad_read = both[:states], both[states:]
-    sums_seq = lax.psum(jnp.concatenate([rates, skip_part], axis=0), "seq")
+    sums_seq = jnp.sum(from_all(jnp.concatenate([rates, skip_part], axis=0), "seq"), axis=0)
     grad_rates, grad_skip = sums_seq[:states], sums_seq[states]
     grad_weight = lax.dot_general(
         gated_all, columns, (((0,), (0,)), ((), ())), preferred_element_type=f32

time: 187 us -> 173 us (0.925)
  blocking collectives: 38.4 us -> 10 us
  starting transfers between devices: 4.58 us -> 25.9 us
  between operations: 13.9 us -> 0.82 us
  local copies, waits for them, and re-layouts: 16.6 us -> 26.7 us
  waiting for transfers between devices: 68 us -> 60.7 us
  other arithmetic: 8.33 us -> 11.6 us
    all_to_all x0 -> x5, waiting for transfers between devices: none -> 51.8 us  [the longest x4 45.9 us: from_all(): return lax.all_to_all(copies, axis, split_axis=0, concat_axis=0, tiled=True)]
    all_gather x2 -> x0, waiting for transfers between devices: 37.2 us -> none  [the longest x1 23 us: on_device(): dout_full = lax.all_gather(out_cotangent, 'chan', axis=1, tiled=True)]
    unnamed x4 -> x0, waiting for transfers between devices: 30.9 us -> none
    psum x1 -> x0, blocking collectives: 24 us -> none  [on_device(): sums_seq = lax.psum(jnp.concatenate([rates, skip_part], axis=0), 'seq')]
    all_to_all x0 -> x5, starting transfers between devices: none -> 21.6 us  [the longest x4 18 us: from_all(): return lax.all_to_all(copies, axis, split_axis=0, concat_axis=0, tiled=True)]
    all_gather x2 -> x0, blocking collectives: 14.4 us -> none  [the longest x1 7.37 us: on_device(): endings = lax.all_gather(ending, 'seq', axis=0)]
    all_to_all x0 -> x1, blocking collectives: none -> 10 us  [from_all(): return lax.all_to_all(copies, axis, split_axis=0, concat_axis=0, tiled=True)]
    all_to_all x1, waiting for transfers between devices: 0.01 us -> 8.85 us  [on_device(): lax.all_to_all(dout_full, 'seq', split_axis=1, concat_axis=0, tiled=True)]
  transfers between devices with their start and end apart: 4 -> 6, of which waited for: 3 -> 6; matrix products, arithmetic and copies ran while one was open for 9% -> 13% of each run, Pallas kernels for 3% -> 0%
where the time goes in v1:
time: 173 us; the launch traced here: 171 us
  waiting for transfers between devices  60.7 us (35%)
  Pallas kernels  28.3 us (16%)
  local copies, waits for them, and re-layouts  26.7 us (15%)
  starting transfers between devices  25.9 us (15%)
  other arithmetic  11.6 us (7%)
  blocking collectives  10 us (6%)
  matrix products  7.44 us (4%)
    all_to_all x4, waiting for transfers between devices, from_all(): return lax.all_to_all(copies, axis, split_axis=0, concat_axis=0, tiled=True)  45.9 us
    all_to_all x4, starting transfers between devices, from_all(): return lax.all_to_all(copies, axis, split_axis=0, concat_axis=0, tiled=True)  18 us
    pallas_call x1, Pallas kernels, on_device(): pl.pallas_call(back_kernel, grid=(nblocks,), in_specs=[by_token] * 4 + [s...  12.1 us
    pallas_call x1, Pallas kernels, on_device(): pl.pallas_call(forward_kernel, grid=(nblocks,), in_specs=[by_token] * 4 +...  11.3 us
    all_to_all x1, blocking collectives, from_all(): return lax.all_to_all(copies, axis, split_axis=0, concat_axis=0, tiled=True)  10 us
    all_to_all x1, waiting for transfers between devices, on_device(): lax.all_to_all(dout_full, 'seq', split_axis=1, concat_axis=0, tiled=True)  8.85 us
    broadcast_in_dim x5, local copies, waits for them, and re-layouts, from_all(): copies = jnp.broadcast_to(array[None], (lax.axis_size(axis),) + array.shape)  6.26 us
    all_to_all x1, waiting for transfers between devices, on_device(): lax.all_to_all(pieces, 'chan', split_axis=0, concat_axis=0, tiled=True)  5.89 us
  transfers between devices with their start and end apart: 6, of which 6 were waited for; matrix products, arithmetic and copies ran while one was open for 13% of the time, Pallas kernels for 0%

profile of v1, /device:TPU:0, one launch (start us, length us, event | category | flops | bytes accessed | tf_op | source)
XLA Modules:
  0.0 171.4 jit_solution(845288849945529615)
XLA Ops:
  3.1 1.9 %broadcast_in_dim.31.b_ref = f32[4096,128]{1,0:T(8,128)} broadcast(f32[4096]{0:T(1024)S(1)} %broadcast_in_dim.30), dimensions={0} | broadcast | bytes 2113536 | tf_op jit(solution)/shard_map/broadcast_in_dim | solution.py:229
  5.1 4.9 %ending.1 = f32[24,640]{1,0:T(8,128)} custom-call(bf16[256,640]{1,0:T(8,128)(2,1)} %raw_ref.5, bf16[256,640]{1,0:T(8,128)(2,1)} %x_ref.5, f32[16,640]{1,0:T(8,128)} %get-tuple-element.53.a2_ref, f32[4096,128]{1,0:T(8,128)} %broadcast_in_dim.31.b_ref), custom_call_target="tpu_custom_call" | custom-call | flops 13107200 | bytes 10485760 | tf_op jit(solution)/shard_map/ending/pallas_call | solution.py:260
  10.8 10.0 %all_to_all.46 = f32[4,24,640]{2,1,0:T(8,128)} all-to-all(f32[4,24,640]{2,1,0:T(8,128)S(1)} %broadcast_in_dim.32), channel_id=1, replica_groups=mesh['seq'=4,'chan'=8] {'seq'}, dimensions={0} | all-to-all | bytes 491520 | tf_op jit(solution)/shard_map/all_to_all | solution.py:29
  21.9 6.3 %all-to-all-start = ((bf16[8,256,320]{1,2,0:T(8,128)(2,1)}), bf16[8,256,320]{1,2,0:T(8,128)(2,1)}, u32[]{:S(2)}, u32[]{:S(2)}) async-start(bf16[8,256,320]{1,2,0:T(8,128)(2,1)} %broadcast_in_dim.25), calls=%async_computation | async-start | bytes 2621440 | tf_op jit(solution)/shard_map/all_to_all | solution.py:29
  30.6 1.8 %compare_select_fusion = (bf16[256,256]{1,0:T(8,128)(2,1)}, bf16[256,256]{1,0:T(8,128)(2,1)}) fusion(bf16[256,256]{1,0:T(8,128)(2,1)} %copy.52, s32[256]{0:T(256)S(1)} %get-tuple-element.59, s32[256]{0:T(256)S(1)} %get-tuple-element.58, bf16[256,256]{1,0:T(8,128)(2,1)} %copy.50), kind=kLoop, calls=%fused_computation.2 | loop fusion | flops 196608 | bytes 526336 | tf_op jit(solution)/shard_map/jit(_where)/select_n | solution.py:234
  34.8 24.6 %all-to-all-done = bf16[8,256,320]{1,2,0:T(8,128)(2,1)} async-done(((bf16[8,256,320]{1,2,0:T(8,128)(2,1)}), bf16[8,256,320]{1,2,0:T(8,128)(2,1)}, u32[]{:S(2)}, u32[]{:S(2)}) %all-to-all-start) | async-done | bytes 1310752 | tf_op jit(solution)/shard_map/all_to_all | solution.py:29
  59.4 3.4 %fusion.16.dg_ref = f32[256,640]{1,0:T(8,128)} fusion(bf16[256,2560]{0,1:T(8,128)(2,1)} %bitcast.1, bf16[640,2560]{1,0:T(8,128)(2,1)S(1)} %copy-done), kind=kOutput, calls=%fused_computation.44 | convolution fusion | flops 838860800 | bytes 5242880 | tf_op jit(solution)/shard_map/dot_general | solution.py:279
  62.8 1.9 %broadcast_in_dim.27.c_ref = f32[4096,128]{1,0:T(8,128)} broadcast(f32[4096]{0:T(1024)S(1)} %broadcast_in_dim.26), dimensions={0} | broadcast | bytes 2113536 | tf_op jit(solution)/shard_map/broadcast_in_dim | solution.py:229
  64.7 11.3 %forward.1 = (bf16[256,640]{1,0:T(8,128)(2,1)}, bf16[256,640]{1,0:T(8,128)(2,1)}, bf16[4096,640]{1,0:T(8,128)(2,1)}, f32[16,1,256]{2,1,0:T(1,128)}, f32[16,640]{1,0:T(8,128)}, /*index=5*/f32[1,640]{1,0:T(1,128)}) custom-call(bf16[256,640]{1,0:T(8,128)(2,1)} %raw_ref.5, bf16[256,640]{1,0:T(8,128)(2,1)} %x_ref.5, bf16[256,640]{1,0:T(8,128)(2,1)} %gate_ref.3, ...), custom_call_target="tpu_custom_call" | custom-call | flops 31457280 | bytes 10485760 | tf_op jit(solution)/shard_map/forward/pallas_call | solution.py:281
  77.5 4.0 %all-to-all-start.2 = ((f32[4,16,640]{2,1,0:T(8,128)}), f32[4,16,640]{2,1,0:T(8,128)}, u32[]{:S(2)}, u32[]{:S(2)}) async-start(f32[4,16,640]{2,1,0:T(8,128)} %broadcast_in_dim.33), calls=%async_computation.2 | async-start | bytes 327680 | tf_op jit(solution)/shard_map/all_to_all | solution.py:29
  83.9 2.5 %all-to-all-done.2 = f32[4,16,640]{2,1,0:T(8,128)} async-done(((f32[4,16,640]{2,1,0:T(8,128)}), f32[4,16,640]{2,1,0:T(8,128)}, u32[]{:S(2)}, u32[]{:S(2)}) %all-to-all-start.2) | async-done | bytes 163872 | tf_op jit(solution)/shard_map/all_to_all | solution.py:29
  87.9 12.1 %backward.1 = (bf16[256,640]{1,0:T(8,128)(2,1)}, bf16[256,640]{1,0:T(8,128)(2,1)}, f32[16,1,256]{2,1,0:T(1,128)}, f32[16,640]{1,0:T(8,128)}) custom-call(bf16[256,640]{1,0:T(8,128)(2,1)} %raw_ref.5, bf16[256,640]{1,0:T(8,128)(2,1)} %x_ref.5, bf16[256,640]{1,0:T(8,128)(2,1)} %gate_ref.3, f32[256,640]{1,0:T(8,128)} %fusion.16.dg_ref, ...), custom_call_target="tpu_custom_call" | custom-call | flops 36700160 | bytes 10485760 | tf_op jit(solution)/shard_map/backward/pallas_call | solution.py:308
  101.8 3.6 %all-to-all-start.4 = ((f32[8,1,1024]{2,1,0:T(1,128)}), f32[8,1,1024]{2,1,0:T(1,128)S(1)}, u32[]{:S(2)}, u32[]{:S(2)}) async-start(f32[8,1,1024]{2,1,0:T(1,128)} %reshape.97), calls=%async_computation.4 | async-start | bytes 65536 | tf_op jit(solution)/shard_map/all_to_all | solution.py:329
  106.2 5.9 %all-to-all-done.4 = f32[8,1,1024]{2,1,0:T(1,128)S(1)} async-done(((f32[8,1,1024]{2,1,0:T(1,128)}), f32[8,1,1024]{2,1,0:T(1,128)S(1)}, u32[]{:S(2)}, u32[]{:S(2)}) %all-to-all-start.4) | async-done | bytes 32800 | tf_op jit(solution)/shard_map/all_to_all | solution.py:329
  112.9 3.4 %all-to-all-start.3 = ((f32[4,17,640]{2,1,0:T(8,128)}), f32[4,17,640]{2,1,0:T(8,128)S(1)}, u32[]{:S(2)}, u32[]{:S(2)}) async-start(f32[4,17,640]{2,1,0:T(8,128)} %broadcast_in_dim.34), calls=%async_computation.3 | async-start | bytes 491520 | tf_op jit(solution)/shard_map/all_to_all | solution.py:29
  116.3 1.9 %copy.57 = bf16[256,640]{0,1:T(8,128)(2,1)} copy(bf16[256,640]{1,0:T(8,128)(2,1)} %get-tuple-element.27) | data formatting | bytes 655360 | tf_op jit(solution)/shard_map/forward/pallas_call | solution.py:281
  118.1 3.9 %all-to-all-done.3 = f32[4,17,640]{2,1,0:T(8,128)S(1)} async-done(((f32[4,17,640]{2,1,0:T(8,128)}), f32[4,17,640]{2,1,0:T(8,128)S(1)}, u32[]{:S(2)}, u32[]{:S(2)}) %all-to-all-start.3) | async-done | bytes 174112 | tf_op jit(solution)/shard_map/all_to_all | solution.py:29
  122.1 2.1 %broadcast_in_dim.35 = bf16[4,256,640]{1,2,0:T(8,128)(2,1)} broadcast(bf16[256,640]{0,1:T(8,128)(2,1)} %copy.57), dimensions={1,2} | broadcast | bytes 1638400 | tf_op jit(solution)/shard_map/broadcast_in_dim | solution.py:28
  124.2 4.3 %all-to-all-start.5 = ((bf16[4,256,640]{1,2,0:T(8,128)(2,1)}), bf16[4,256,640]{1,2,0:T(8,128)(2,1)}, u32[]{:S(2)}, u32[]{:S(2)}) async-start(bf16[4,256,640]{1,2,0:T(8,128)(2,1)} %broadcast_in_dim.35), calls=%async_computation.5 | async-start | bytes 2621440 | tf_op jit(solution)/shard_map/all_to_all | solution.py:29
  128.5 2.4 %copy.58 = bf16[256,4,640]{2,0,1:T(8,128)(2,1)} copy(bf16[256,4,640]{0,2,1:T(8,128)(2,1)} %bitcast.18) | data formatting | bytes 2621440 | tf_op jit(solution)/shard_map/all_to_all | solution.py:302
  130.9 14.9 %all-to-all-done.5 = bf16[4,256,640]{1,2,0:T(8,128)(2,1)} async-done(((bf16[4,256,640]{1,2,0:T(8,128)(2,1)}), bf16[4,256,640]{1,2,0:T(8,128)(2,1)}, u32[]{:S(2)}, u32[]{:S(2)}) %all-to-all-start.5) | async-done | bytes 1310752 | tf_op jit(solution)/shard_map/all_to_all | solution.py:29
  145.8 4.3 %all-to-all-start.6 = ((bf16[256,4,640]{2,0,1:T(8,128)(2,1)}), bf16[256,4,640]{2,0,1:T(8,128)(2,1)}, u32[]{:S(2)}, u32[]{:S(2)}) async-start(bf16[256,4,640]{2,0,1:T(8,128)(2,1)} %copy.58), calls=%async_computation.6 | async-start | bytes 2621440 | tf_op jit(solution)/shard_map/all_to_all | solution.py:302
  158.5 8.9 %all-to-all-done.6 = bf16[256,4,640]{2,0,1:T(8,128)(2,1)} async-done(((bf16[256,4,640]{2,0,1:T(8,128)(2,1)}), bf16[256,4,640]{2,0,1:T(8,128)(2,1)}, u32[]{:S(2)}, u32[]{:S(2)}) %all-to-all-start.6) | async-done | bytes 1310752 | tf_op jit(solution)/shard_map/all_to_all | solution.py:302
  167.4 4.1 %convolution_bitcast_fusion = f32[640,640]{1,0:T(8,128)} fusion(bf16[4,256,640]{1,2,0:T(8,128)(2,1)} %all-to-all-done.5, bf16[256,4,640]{2,0,1:T(8,128)(2,1)} %all-to-all-done.6), kind=kOutput, calls=%fused_computation | convolution fusion | flops 838860800 | bytes 4259840 | tf_op jit(solution)/shard_map/dot_general | solution.py:333
  (58 shorter events, 26.3 us)
Async XLA Ops:
  0.6 58.8 %copy-start = (bf16[640,2560]{1,0:T(8,128)(2,1)S(1)}, bf16[640,2560]{1,0:T(8,128)(2,1)}, u32[]{:S(2)}) copy-start(bf16[640,2560]{1,0:T(8,128)(2,1)} %param.16) | copy-start | bytes 9830404
  5.1 15.7 %copy-start.2 = (bf16[256,320]{0,1:T(8,128)(2,1)S(1)}, bf16[256,320]{0,1:T(8,128)(2,1)}, u32[]{:S(2)}) copy-start(bf16[256,320]{0,1:T(8,128)(2,1)} %param.17) | copy-start | bytes 491524
  21.9 6.3 %copy-start.4 = (f32[16,256]{1,0:T(8,128)S(1)}, f32[16,256]{1,0:T(8,128)}, u32[]{:S(2)}) copy-start(f32[16,256]{1,0:T(8,128)} %param.15) | copy-start | bytes 49156
  21.9 7.3 %copy-start.5 = (f32[16,256]{1,0:T(8,128)S(1)}, f32[16,256]{1,0:T(8,128)}, u32[]{:S(2)}) copy-start(f32[16,256]{1,0:T(8,128)} %param.14) | copy-start | bytes 49156
  21.9 8.1 %copy-start.6 = (f32[640]{0:T(1024)S(1)}, f32[640]{0:T(1024)}, u32[]{:S(2)}) copy-start(f32[640]{0:T(1024)} %param.13) | copy-start | bytes 7684
  21.9 37.5 %all-to-all-start = ((bf16[8,256,320]{1,2,0:T(8,128)(2,1)}), bf16[8,256,320]{1,2,0:T(8,128)(2,1)}, u32[]{:S(2)}, u32[]{:S(2)}) async-start(bf16[8,256,320]{1,2,0:T(8,128)(2,1)} %broadcast_in_dim.25), calls=%async_computation | async-start | bytes 2621440 | tf_op jit(solution)/shard_map/all_to_all | solution.py:29
  28.2 5.0 %copy-start.1 = (f32[16,640]{1,0:T(8,128)S(1)}, f32[16,640]{1,0:T(8,128)}, u32[]{:S(2)}) copy-start(f32[16,640]{1,0:T(8,128)} %get-tuple-element.53.a2_ref) | copy-start | bytes 122884
  77.5 9.0 %all-to-all-start.2 = ((f32[4,16,640]{2,1,0:T(8,128)}), f32[4,16,640]{2,1,0:T(8,128)}, u32[]{:S(2)}, u32[]{:S(2)}) async-start(f32[4,16,640]{2,1,0:T(8,128)} %broadcast_in_dim.33), calls=%async_computation.2 | async-start | bytes 327680 | tf_op jit(solution)/shard_map/all_to_all | solution.py:29
  87.9 17.6 %copy-start.7 = (f32[1,640]{1,0:T(1,128)S(1)}, f32[1,640]{1,0:T(1,128)}, u32[]{:S(2)}) copy-start(f32[1,640]{1,0:T(1,128)} %get-tuple-element.24) | copy-start | bytes 7684
  101.8 10.3 %all-to-all-start.4 = ((f32[8,1,1024]{2,1,0:T(1,128)}), f32[8,1,1024]{2,1,0:T(1,128)S(1)}, u32[]{:S(2)}, u32[]{:S(2)}) async-start(f32[8,1,1024]{2,1,0:T(1,128)} %reshape.97), calls=%async_computation.4 | async-start | bytes 65536 | tf_op jit(solution)/shard_map/all_to_all | solution.py:329
  112.1 0.7 copy-start.3
  112.9 9.2 %all-to-all-start.3 = ((f32[4,17,640]{2,1,0:T(8,128)}), f32[4,17,640]{2,1,0:T(8,128)S(1)}, u32[]{:S(2)}, u32[]{:S(2)}) async-start(f32[4,17,640]{2,1,0:T(8,128)} %broadcast_in_dim.34), calls=%async_computation.3 | async-start | bytes 491520 | tf_op jit(solution)/shard_map/all_to_all | solution.py:29
  124.2 21.6 %all-to-all-start.5 = ((bf16[4,256,640]{1,2,0:T(8,128)(2,1)}), bf16[4,256,640]{1,2,0:T(8,128)(2,1)}, u32[]{:S(2)}, u32[]{:S(2)}) async-start(bf16[4,256,640]{1,2,0:T(8,128)(2,1)} %broadcast_in_dim.35), calls=%async_computation.5 | async-start | bytes 2621440 | tf_op jit(solution)/shard_map/all_to_all | solution.py:29
  145.8 21.6 %all-to-all-start.6 = ((bf16[256,4,640]{2,0,1:T(8,128)(2,1)}), bf16[256,4,640]{2,0,1:T(8,128)(2,1)}, u32[]{:S(2)}, u32[]{:S(2)}) async-start(bf16[256,4,640]{2,0,1:T(8,128)(2,1)} %copy.58), calls=%async_computation.6 | async-start | bytes 2621440 | tf_op jit(solution)/shard_map/all_to_all | solution.py:302
